TPU v7x, 32 devices: a whole 2x2x4 slice. The times are simulated.
32 devices in a mesh: req: 4 (over z), head: 2 (over core), exp: 4 (over y, x).
Axes of the slice: x: 2, y: 2, z: 4, core: 2. Of those that a mesh axis runs over, the one named last changes fastest.
Arguments:
- queries: bfloat16 [16, 64, 32, 128], P('req', 'exp', 'head'), may hold values from -8 to 8
- new_keys: bfloat16 [16, 64, 4, 128], P('req', 'exp', 'head'), may hold values from -8 to 8
- new_values: bfloat16 [16, 64, 4, 128], P('req', 'exp', 'head'), may hold values from -6 to 6
- key_cache: bfloat16 [16, 24576, 4, 128], P('req', 'exp', 'head'), may hold values from -6 to 6
- value_cache: bfloat16 [16, 24576, 4, 128], P('req', 'exp', 'head'), may hold values from -6 to 6
- lengths: int32 [16], P('req'), may hold values from 1 to 24576, 131072 in all
- residual: bfloat16 [1024, 2048], P(('req', 'exp')), may hold values from -24 to 24
- out_weight: bfloat16 [4096, 2048], P('head', 'exp'), may hold values from -1.796875 to 1.796875
- norm_gain: float32 [2048], replicated, may hold values from 0.1 to 1.9
- route_ids: int32 [1024, 8], P(('req', 'exp')), may hold values from 0 to 15, all different within a row; in each aligned block of 64 rows (0 to 63, 64 to 127, ...) at most 64 rows name the same one
- route_weights: float32 [1024, 8], P(('req', 'exp')), may hold values from 0.05 to 0.3
- expert_in: bfloat16 [16, 2048, 2, 768], P(('req', 'exp'), None, None, 'head'), may hold values from -0.125 to 0.125
- expert_out: bfloat16 [16, 768, 2048], P(('req', 'exp'), 'head'), may hold values from -0.21875 to 0.21875
Outputs:
- output: bfloat16 [1024, 2048], P(('req', 'exp'), 'head')
Inputs may be any that keep to these rules, and one draw needn't show every extreme that they name: `route_ids`: each row names 8 different experts. Among the 64 rows of one device (aligned blocks of rows 0 to 63, 64 to 127 and so on) no expert is named by more than 64 rows.
All inputs are finite; a program needn't handle non-finite values. No bound on the sum of `lengths` on one device may be relied on, other than what follows from the above.
Results may differ from a plain program's by a relative error of at most 0.0051.
Values may be sent and summed in bfloat16 or wider, within the bound.
No kernel may reach another device: no remote copies, remote signals or barrier semaphores. Data moves between devices by JAX's collectives and lax.ppermute only.
A program may use at most 192 MiB of HBM per device.

v0:
```python
import jax
import jax.numpy as jnp
from jax import lax
from jax.sharding import PartitionSpec as P

masked_score = -1e30
norm_epsilon = 1e-06


def normalize(value_sums, row_totals, heads_local):
    lead = value_sums.shape[:2]
    shaped = value_sums.reshape(lead[0], lead[1], heads_local, -1) / row_totals[..., None]
    return shaped.reshape(lead[0], lead[1], -1).astype(jnp.bfloat16)


def local(
    queries,
    new_keys,
    new_values,
    key_cache,
    value_cache,
    lengths,
    residual,
    out_weight,
    norm_gain,
    route_ids,
    route_weights,
    expert_in,
    expert_out,
):
    req_count, cache_span, kv_local, head_size = key_cache.shape
    heads_local = queries.shape[2]
    group_size = heads_local // kv_local
    score_scale = head_size ** (-0.5)
    whole_queries = lax.all_gather(queries, "exp", axis=1, tiled=True)
    block_rows = whole_queries.shape[1]
    grouped = whole_queries.reshape(req_count, block_rows, kv_local, group_size, head_size)
    cache_scores = (
        jnp.einsum("rbkgd,rskd->rkgbs", grouped, key_cache, preferred_element_type=jnp.float32)
        * score_scale
    )
    fresh_scores = (
        jnp.einsum("rbkgd,rnkd->rkgbn", grouped, new_keys, preferred_element_type=jnp.float32)
        * score_scale
    )
    positions = lax.axis_index("exp") * cache_span + lax.iota(jnp.int32, cache_span)
    valid_cache = positions[None, :] < lengths[:, None]
    cache_scores = jnp.where(valid_cache[:, None, None, None, :], cache_scores, masked_score)
    local_max = jnp.maximum(jnp.max(cache_scores, axis=-1), jnp.max(fresh_scores, axis=-1))
    row_max = lax.pmax(local_max, "exp")
    cache_exp = jnp.exp(cache_scores - row_max[..., None])
    fresh_exp = jnp.exp(fresh_scores - row_max[..., None])
    totals = jnp.sum(cache_exp, axis=-1) + jnp.sum(fresh_exp, axis=-1)
    weighted = jnp.einsum(
        "rkgbs,rskd->rbkgd",
        cache_exp.astype(jnp.bfloat16),
        value_cache,
        preferred_element_type=jnp.float32,
    )
    weighted = weighted + jnp.einsum(
        "rkgbn,rnkd->rbkgd",
        fresh_exp.astype(jnp.bfloat16),
        new_values,
        preferred_element_type=jnp.float32,
    )
    weighted = weighted.reshape(req_count, block_rows, heads_local * head_size)
    totals = jnp.transpose(totals, (0, 3, 1, 2)).reshape(req_count, block_rows, heads_local)
    all_sums, all_totals = lax.psum((weighted, totals), "exp")
    merged = normalize(all_sums, all_totals, heads_local)
    projected = jnp.dot(
        merged.reshape(req_count * block_rows, -1), out_weight, preferred_element_type=jnp.float32
    )
    projected = projected.reshape(req_count, block_rows, -1)
    projected = lax.psum(projected, "head")
    projected = projected.reshape(req_count * block_rows, projected.shape[-1])
    attn_out = lax.all_to_all(projected, "exp", split_axis=0, concat_axis=1, tiled=True)
    hidden = residual.astype(jnp.float32) + attn_out
    normed = (
        hidden
        * lax.rsqrt(jnp.mean(hidden * hidden, axis=-1, keepdims=True) + norm_epsilon)
        * norm_gain
    ).astype(jnp.bfloat16)
    row_count, model_width = normed.shape
    top_count = route_ids.shape[1]
    local_experts = expert_in.shape[0]
    groups = lax.axis_size("req") * lax.axis_size("exp")
    experts_all = local_experts * groups
    capacity = max(2, 2 * row_count * top_count // experts_all)
    expert_iota = lax.iota(jnp.int32, experts_all)
    named_count = jnp.sum((route_ids[:, :, None] == expert_iota).astype(jnp.int32), axis=1)
    earlier = jnp.cumsum(named_count, axis=0) - named_count
    slot_rank = jnp.take_along_axis(earlier, route_ids, axis=1)
    slot_index = route_ids * capacity + slot_rank
    slot_iota = lax.iota(jnp.int32, experts_all * capacity)
    placing = jnp.any(slot_index[None, :, :] == slot_iota[:, None, None], axis=2).astype(
        jnp.bfloat16
    )
    outgoing = jnp.dot(placing, normed, preferred_element_type=jnp.float32).astype(jnp.bfloat16)
    outgoing = outgoing.reshape(groups, local_experts, capacity, model_width)
    input_maps = expert_in.reshape(local_experts, model_width, -1)
    gate_up = jnp.einsum(
        "geci,eif->gecf",
        lax.all_to_all(outgoing, ("req", "exp"), split_axis=0, concat_axis=0, tiled=True),
        input_maps,
        preferred_element_type=jnp.float32,
    )
    half_units = gate_up.shape[-1] // 2
    activated = (jax.nn.silu(gate_up[..., :half_units]) * gate_up[..., half_units:]).astype(
        jnp.bfloat16
    )
    partial_value = jnp.einsum(
        "gecf,efi->geci", activated, expert_out, preferred_element_type=jnp.float32
    )
    half_width = model_width // lax.axis_size("head")
    head_start = lax.axis_index("head") * half_width
    summed = lax.psum_scatter(partial_value, "head", scatter_dimension=3, tiled=True).astype(
        jnp.bfloat16
    )
    returned = lax.all_to_all(summed, ("req", "exp"), split_axis=0, concat_axis=0, tiled=True)
    flat_results = returned.reshape(experts_all * capacity, half_width)
    picked = jnp.take(flat_results, slot_index, axis=0).astype(jnp.float32)
    mixture = jnp.sum(picked * route_weights[:, :, None], axis=1)
    kept_hidden = lax.dynamic_slice_in_dim(hidden, head_start, half_width, 1)
    return (kept_hidden + mixture).astype(jnp.bfloat16)


def solution(mesh):
    return jax.shard_map(
        local,
        mesh=mesh,
        in_specs=(
            P("req", "exp", "head", None),
            P("req", "exp", "head", None),
            P("req", "exp", "head", None),
            P("req", "exp", "head", None),
            P("req", "exp", "head", None),
            P("req"),
            P(("req", "exp"), None),
            P("head", "exp"),
            P(),
            P(("req", "exp"), None),
            P(("req", "exp"), None),
            P(("req", "exp"), None, None, "head"),
            P(("req", "exp"), "head", None),
        ),
        out_specs=P(("req", "exp"), "head"),
        check_vma=False,
    )
```

profile of v0, /device:TPU:12, one launch (start us, length us, event | category | flops | bytes accessed | tf_op | source)
XLA Modules:
  0.0 454.6 jit_solution(866792332036703675)
XLA Ops:
  6.5 0.0 copy-start
  6.5 0.0 all-gather.2.cloned.1.call-start
  6.5 0.7 all-gather.2.cloned.1.call-update
  7.3 0.0 all-reduce.3.cloned.1.call-start
  7.3 0.8 broadcast_compare_fusion
  8.1 28.7 %all-gather.2.cloned.1.call-done = bf16[4,64,16,128]{3,2,1,0:T(8,128)(2,1)} async-done(((bf16[4,16,16,128]{3,2,1,0:T(8,128)(2,1)}), bf16[4,64,16,128]{3,2,1,0:T(8,128)(2,1)}) %all-gather.2.cloned.1.call-update) | async-done | bytes 1048592 | tf_op jit(solution)/shard_map/all_gather | solution.py:35
  36.8 1.5 copy.79
  38.3 2.5 fusion.33
  40.8 43.4 %bitcast_reduce_fusion = (f32[4,2,8,64]{3,2,1,0:T(8,128)S(1)}, f32[4,2,6144,64,8]{2,3,4,1,0:T(8,128)}) fusion(pred[4,6144]{1,0:T(4,128)(4,1)S(1)} %broadcast_compare_fusion, bf16[4,64,2,8,128]{4,1,3,2,0:T(8,128)(2,1)S(1)} %bitcast.78, bf16[4,6144,2,128,1]{3,2,1,0,4:T(2,128)(2,1)} %bitcast.76), kind=kOutput, calls=%fused_computation.3 | convolution fusion | flops 6517944320 | bytes 114335744 | tf_op jit(solution)/shard_map/rbkgd,rskd->rkgbs/dot_general | solution.py:39
  84.2 15.3 %pmax.7 = f32[4,2,8,64]{3,2,1,0:T(8,128)S(1)} all-reduce(f32[4,2,8,64]{3,2,1,0:T(8,128)S(1)} %max.5), channel_id=1, replica_groups=mesh['req'=4,'head'=2,'exp'=4] {'exp'}, use_global_device_ids=true, to_apply=%region_2.3 | all-reduce | flops 4096 | bytes 32768 | tf_op jit(solution)/shard_map/pmax | solution.py:50
  99.5 0.0 copy-start.1
  99.5 0.0 copy-start.5
  99.5 38.4 %fusion.3 = f32[4,2,8,64,128]{4,3,2,1,0:T(8,128)} fusion(f32[4,2,6144,64,8]{2,3,4,1,0:T(8,128)} %get-tuple-element.10, f32[4,2,8,64]{3,2,1,0:T(8,128)S(1)} %pmax.7, pred[4,6144]{1,0:T(4,128)(4,1)S(1)} %broadcast_compare_fusion, bf16[4,6144,2,128,1]{3,2,1,0,4:T(2,128)(2,1)} %bitcast.83), kind=kOutput, calls=%fused_computation.8 | convolution fusion | flops 6543114240 | bytes 115384320 | tf_op jit(solution)/shard_map/rkgbs,rskd->rbkgd/dot_general | solution.py:54
  138.0 2.1 add_bitcast_fusion
  140.1 2.5 copy.84
  142.6 2.7 reshape.99
  145.3 0.0 all-reduce.3.cloned.1.call-update
  145.3 0.0 all-reduce.5.cloned.1.call-start
  145.4 32.4 %fusion.1 = f32[4,2,8,64]{3,2,1,0:T(8,128)S(1)} fusion(f32[4,2,6144,64,8]{2,3,4,1,0:T(8,128)} %get-tuple-element.10, f32[4,2,8,64]{3,2,1,0:T(8,128)S(1)} %pmax.7, pred[4,6144]{1,0:T(4,128)(4,1)S(1)} %broadcast_compare_fusion), kind=kLoop, calls=%fused_computation.6 | loop fusion | flops 100659200 | bytes 100720640 | tf_op jit(solution)/shard_map/reduce_sum | solution.py:53
  177.8 0.2 fusion.22
  177.9 14.9 %psum.22 = f32[4,64,16]{1,2,0:T(8,128)S(1)} all-reduce(f32[4,64,16]{1,2,0:T(8,128)S(1)} %add_bitcast_fusion.1), channel_id=1, replica_groups=mesh['req'=4,'head'=2,'exp'=4] {'exp'}, use_global_device_ids=true, to_apply=%region_6.7 | all-reduce | flops 4096 | bytes 32768 | tf_op jit(solution)/shard_map/psum | solution.py:68
  192.8 0.1 copy.85
  192.9 1.9 div.21
  194.8 2.7 div.22
  197.6 17.7 %all-reduce.3.cloned.1.call-done = f32[4,64,2048]{2,1,0:T(8,128)} async-done(((f32[4,64,2048]{2,1,0:T(8,128)}), f32[4,64,2048]{2,1,0:T(8,128)}) %all-reduce.3.cloned.1.call-update) | async-done | bytes 2097168 | tf_op jit(solution)/shard_map/psum | solution.py:68
  215.3 0.0 copy-done
  215.3 3.7 fusion.11
  219.0 0.0 all-reduce.5.cloned.1.call-update
  219.1 19.2 %all-reduce.5.cloned.1.call-done = f32[4,64,512]{2,1,0:T(8,128)} async-done(((f32[4,64,512]{2,1,0:T(8,128)}), f32[4,64,512]{2,1,0:T(8,128)}) %all-reduce.5.cloned.1.call-update) | async-done | bytes 524304 | tf_op jit(solution)/shard_map/psum | solution.py:74
  238.2 4.2 all-to-all-start
  242.4 0.1 copy.87
  242.5 0.1 reduce_window_sum.11
  242.6 0.1 copy.89
  242.7 0.1 reshape.116
  242.8 0.0 copy-start.3
  242.8 0.0 copy-start.6
  242.8 3.8 gather_fusion.1
  246.6 0.1 reshape.119
  246.7 0.1 copy.90
  246.8 0.1 copy.92
  246.9 0.7 fusion.13
  247.6 2.8 all-to-all-done
  250.4 0.0 copy-done.3
  250.4 0.2 multiply_reduce_fusion.1
  250.6 0.8 copy-done.2
  251.4 3.3 convolution_convert_fusion
  254.7 6.1 %all-to-all-start.1 = ((bf16[16,1,64,2048]{3,2,1,0:T(8,128)(2,1)}), bf16[16,1,64,2048]{3,2,1,0:T(8,128)(2,1)}, u32[]{:S(2)}, u32[]{:S(2)}) async-start(bf16[16,1,64,2048]{3,2,1,0:T(8,128)(2,1)} %bitcast.75), calls=%async_computation.1 | async-start | bytes 8388608 | tf_op jit(solution)/shard_map/all_to_all | solution.py:103
  260.8 0.0 reduce-scatter.2.cloned.1.call-start
  260.8 8.1 %reshape.134 = bf16[2048,768,1]{1,0,2:T(8,128)(2,1)} reshape(bf16[1,2048,2,384]{3,2,1,0:T(2,128)(2,1)} %param.24) | data formatting | bytes 6291456 | tf_op jit(solution)/shard_map/reshape.3
  268.9 84.6 %all-to-all-done.1 = bf16[16,1,64,2048]{3,2,1,0:T(8,128)(2,1)} async-done(((bf16[16,1,64,2048]{3,2,1,0:T(8,128)(2,1)}), bf16[16,1,64,2048]{3,2,1,0:T(8,128)(2,1)}, u32[]{:S(2)}, u32[]{:S(2)}) %all-to-all-start.1) | async-done | bytes 4194336 | tf_op jit(solution)/shard_map/all_to_all | solution.py:103
  353.5 6.3 %fusion.14 = f32[16,1,64,768]{3,2,0,1:T(8,128)S(1)} fusion(bf16[2048,768,1]{1,0,2:T(8,128)(2,1)} %reshape.134, bf16[16,1,64,2048]{3,2,1,0:T(8,128)(2,1)} %all-to-all-done.1), kind=kOutput, calls=%fused_computation.25 | convolution fusion | flops 3221225472 | bytes 10485760 | tf_op jit(solution)/shard_map/geci,eif->gecf/dot_general | solution.py:101
  359.8 5.6 %convolution_bitcast_fusion = f32[16,1,64,2048]{3,2,0,1:T(8,128)} fusion(bf16[1,384,2048]{2,1,0:T(8,128)(2,1)S(1)} %copy-done.8, f32[16,1,64,768]{3,2,0,1:T(8,128)S(1)} %fusion.14), kind=kOutput, calls=%fused_computation.13 | convolution fusion | flops 1612972032 | bytes 13107200 | tf_op jit(solution)/shard_map/gecf,efi->geci/dot_general | solution.py:111
  365.4 0.0 reduce-scatter.2.cloned.1.call-update
  365.4 16.2 %reduce-scatter.2.cloned.1.call-done = f32[16,1,64,1024]{3,2,0,1:T(8,128)} async-done(((f32[16,1,64,2048]{3,2,0,1:T(8,128)}), f32[16,1,64,1024]{3,2,0,1:T(8,128)}) %reduce-scatter.2.cloned.1.call-update) | async-done | bytes 4194320 | tf_op jit(solution)/shard_map/reduce_scatter | solution.py:116
  381.6 3.9 convert_bitcast_fusion
  385.5 7.1 %all-to-all-start.2 = ((bf16[16,1,64,1024]{3,2,1,0:T(8,128)(2,1)}), bf16[16,1,64,1024]{3,2,1,0:T(8,128)(2,1)}, u32[]{:S(2)}, u32[]{:S(2)}) async-start(bf16[16,1,64,1024]{3,2,1,0:T(8,128)(2,1)} %convert_bitcast_fusion), calls=%async_computation.3 | async-start | bytes 4194304 | tf_op jit(solution)/shard_map/all_to_all | solution.py:119
  392.6 0.1 copy.95
  392.7 0.1 reshape.110
  392.8 0.1 copy.91
  392.9 0.1 copy.96
  393.0 48.1 %all-to-all-done.2 = bf16[16,1,64,1024]{3,2,1,0:T(8,128)(2,1)} async-done(((bf16[16,1,64,1024]{3,2,1,0:T(8,128)(2,1)}), bf16[16,1,64,1024]{3,2,1,0:T(8,128)(2,1)}, u32[]{:S(2)}, u32[]{:S(2)}) %all-to-all-start.2) | async-done | bytes 2097184 | tf_op jit(solution)/shard_map/all_to_all | solution.py:119
  441.0 4.6 %gather_fusion = bf16[512,1024]{1,0:T(8,128)(2,1)S(1)} fusion(bf16[1024,1024]{1,0:T(8,128)(2,1)} %bitcast.28, s32[1024]{0:T(1024)S(1)} %pad_clamp_fusion), kind=kCustom, calls=%fused_computation | custom fusion | bytes 2099200 | tf_op jit(solution)/shard_map/jit(_take)/gather | solution.py:121
  445.6 0.8 multiply_reduce_fusion
  446.5 1.6 add_convert_fusion
  (21 shorter events, 0.1 us)
Async XLA Ops:
  6.5 208.7 %copy-start = (bf16[2048,512]{1,0:T(8,128)(2,1)S(1)}, bf16[2048,512]{1,0:T(8,128)(2,1)}, u32[]{:S(2)}) copy-start(bf16[2048,512]{1,0:T(8,128)(2,1)} %param.20) | copy-start | bytes 6291460
  6.5 30.3 %all-gather.2.cloned.1.call-start = ((), (), s32[]{:S(2)}) async-start(), calls=%async_computation.4 | async-start | bytes 1310720 | tf_op jit(solution)/shard_map/all_gather | solution.py:35
  7.3 208.0 %all-reduce.3.cloned.1.call-start = ((), (), s32[]{:S(2)}) async-start(), calls=%async_computation.5 | async-start | bytes 4194304 | tf_op jit(solution)/shard_map/psum | solution.py:68
  99.5 38.4 %copy-start.1 = (f32[4,2,8,64,16]{3,4,2,1,0:T(8,128)S(1)}, f32[4,2,8,64,16]{3,4,2,1,0:T(8,128)}, u32[]{:S(2)}) copy-start(f32[4,2,8,64,16]{3,4,2,1,0:T(8,128)} %get-tuple-element.12) | copy-start | bytes 786436
  99.5 38.4 %copy-start.5 = (bf16[4,16,2,128]{3,2,1,0:T(2,128)(2,1)S(1)}, bf16[4,16,2,128]{3,2,1,0:T(2,128)(2,1)}, u32[]{:S(2)}) copy-start(bf16[4,16,2,128]{3,2,1,0:T(2,128)(2,1)} %param.15) | copy-start | bytes 98308
  145.3 92.9 %all-reduce.5.cloned.1.call-start = ((), (), s32[]{:S(2)}) async-start(), calls=%async_computation.6 | async-start | bytes 1048576 | tf_op jit(solution)/shard_map/psum | solution.py:74
  197.6 21.5 %copy-start.4 = (s32[64,8]{0,1:T(8,128)S(1)}, s32[64,8]{0,1:T(8,128)}, u32[]{:S(2)}) copy-start(s32[64,8]{0,1:T(8,128)} %param.22) | copy-start | bytes 6148
  238.2 12.2 %all-to-all-start = ((f32[4,64,512]{2,1,0:T(8,128)}), f32[4,64,512]{2,1,0:T(8,128)S(1)}, u32[]{:S(2)}, u32[]{:S(2)}) async-start(f32[4,64,512]{2,1,0:T(8,128)} %all-reduce.5.cloned.1.call-done), calls=%async_computation | async-start | bytes 1048576 | tf_op jit(solution)/shard_map/all_to_all | solution.py:76
  242.8 7.6 %copy-start.3 = (bf16[64,2048]{1,0:T(8,128)(2,1)S(1)}, bf16[64,2048]{1,0:T(8,128)(2,1)}, u32[]{:S(2)}) copy-start(bf16[64,2048]{1,0:T(8,128)(2,1)} %param.19) | copy-start | bytes 786436
  242.8 8.6 %copy-start.6 = (f32[2048]{0:T(1024)S(1)}, f32[2048]{0:T(1024)}, u32[]{:S(2)}) copy-start(f32[2048]{0:T(1024)} %param.21) | copy-start | bytes 24580
  250.6 0.8 copy-start.2
  254.7 98.8 %all-to-all-start.1 = ((bf16[16,1,64,2048]{3,2,1,0:T(8,128)(2,1)}), bf16[16,1,64,2048]{3,2,1,0:T(8,128)(2,1)}, u32[]{:S(2)}, u32[]{:S(2)}) async-start(bf16[16,1,64,2048]{3,2,1,0:T(8,128)(2,1)} %bitcast.75), calls=%async_computation.1 | async-start | bytes 8388608 | tf_op jit(solution)/shard_map/all_to_all | solution.py:103
  260.8 120.8 %reduce-scatter.2.cloned.1.call-start = ((), (), s32[]{:S(2)}) async-start(), calls=%async_computation.7 | async-start | bytes 12582912 | tf_op jit(solution)/shard_map/reduce_scatter | solution.py:116
  353.5 6.3 %copy-start.8 = (bf16[1,384,2048]{2,1,0:T(8,128)(2,1)S(1)}, bf16[1,384,2048]{2,1,0:T(8,128)(2,1)}, u32[]{:S(2)}) copy-start(bf16[1,384,2048]{2,1,0:T(8,128)(2,1)} %param.25) | copy-start | bytes 4718596
  385.5 7.4 %copy-start.7 = (f32[64,8]{0,1:T(8,128)S(1)}, f32[64,8]{0,1:T(8,128)}, u32[]{:S(2)}) copy-start(f32[64,8]{0,1:T(8,128)} %param.23) | copy-start | bytes 6148
  385.5 55.6 %all-to-all-start.2 = ((bf16[16,1,64,1024]{3,2,1,0:T(8,128)(2,1)}), bf16[16,1,64,1024]{3,2,1,0:T(8,128)(2,1)}, u32[]{:S(2)}, u32[]{:S(2)}) async-start(bf16[16,1,64,1024]{3,2,1,0:T(8,128)(2,1)} %convert_bitcast_fusion), calls=%async_computation.3 | async-start | bytes 4194304 | tf_op jit(solution)/shard_map/all_to_all | solution.py:119
Sparse Core Ops, SparseCore 0:
  9.2 27.5 all-gather.1
  145.4 69.7 all-reduce.2
  219.2 19.0 all-reduce.4
  365.6 15.9 reduce-scatter.1
where the time goes:
time: 456 us; the launch traced here: 455 us
  waiting for transfers between devices  218 us (48%)
  matrix products  105 us (23%)
  other arithmetic  40.7 us (9%)
  blocking collectives  30.2 us (7%)
  local copies, waits for them, and re-layouts  29.6 us (6%)
  starting transfers between devices  17.5 us (4%)
  between operations  13.3 us (3%)
    all_to_all x1, waiting for transfers between devices, local(): lax.all_to_all(outgoing, ('req', 'exp'), split_axis=0, concat_axis=0, til...  84.6 us
    all_to_all x1, waiting for transfers between devices, local(): lax.all_to_all(summed, ('req', 'exp'), split_axis=0, concat_axis=0, tiled...  48.1 us
    dot_general x1, matrix products, local(): jnp.einsum('rbkgd,rskd->rkgbs', grouped, key_cache, preferred_element_typ...  43.4 us
    dot_general x1, matrix products, local(): jnp.einsum('rkgbs,rskd->rbkgd', cache_exp.astype(jnp.bfloat16), value_cac...  38.4 us
    reduce_sum x2, other arithmetic, local(): totals = jnp.sum(cache_exp, axis=-1) + jnp.sum(fresh_exp, axis=-1)  32.6 us
    all_gather x1, waiting for transfers between devices, local(): whole_queries = lax.all_gather(queries, 'exp', axis=1, tiled=True)  28.7 us
    psum x1, waiting for transfers between devices, local(): projected = lax.psum(projected, 'head')  19.2 us
    psum x1, waiting for transfers between devices, local(): all_sums, all_totals = lax.psum((weighted, totals), 'exp')  17.7 us
  transfers between devices with their start and end apart: 7, of which 7 were waited for; matrix products, arithmetic and copies ran while one was open for 11% of the time, Pallas kernels for 0%

commit v1 on v0

--- a/solution.py
+++ b/solution.py
@@ -32,7 +32,9 @@
     heads_local = queries.shape[2]
     group_size = heads_local // kv_local
     score_scale = head_size ** (-0.5)
-    whole_queries = lax.all_gather(queries, "exp", axis=1, tiled=True)
+    whole_queries = jnp.concatenate(
+        lax.all_to_all(jnp.stack([queries] * lax.axis_size("exp")), "exp", 0, 0), axis=1
+    )
     block_rows = whole_queries.shape[1]
     grouped = whole_queries.reshape(req_count, block_rows, kv_local, group_size, head_size)
     cache_scores = (

time: 456 us -> 445 us (0.976)
  waiting for transfers between devices: 218 us -> 202 us
    all_gather x1 -> x0, waiting for transfers between devices: 28.7 us -> none  [local(): whole_queries = lax.all_gather(queries, 'exp', axis=1, tiled=True)]
    all_to_all x0 -> x1, waiting for transfers between devices: none -> 13 us  [local(): lax.all_to_all(jnp.stack([queries] * lax.axis_size('exp')), 'exp', 0, 0)]
    another operation x1 -> x2, local copies, waits for them, and re-layouts: 8.06 us -> 9.25 us
where the time goes in v1:
time: 445 us
  waiting for transfers between devices  202 us (45%)
  matrix products  105 us (24%)
  other arithmetic  40 us (9%)
  local copies, waits for them, and re-layouts  33 us (7%)
  blocking collectives  30.2 us (7%)
  starting transfers between devices  21.8 us (5%)
  between operations  13.3 us (3%)
    all_to_all x1, waiting for transfers between devices, local(): lax.all_to_all(outgoing, ('req', 'exp'), split_axis=0, concat_axis=0, til...  84.6 us
    all_to_all x1, waiting for transfers between devices, local(): lax.all_to_all(summed, ('req', 'exp'), split_axis=0, concat_axis=0, tiled...  48.1 us
    dot_general x1, matrix products, local(): jnp.einsum('rbkgd,rskd->rkgbs', grouped, key_cache, preferred_element_typ...  43.4 us
    dot_general x1, matrix products, local(): jnp.einsum('rkgbs,rskd->rbkgd', cache_exp.astype(jnp.bfloat16), value_cac...  38.4 us
    reduce_sum x2, other arithmetic, local(): totals = jnp.sum(cache_exp, axis=-1) + jnp.sum(fresh_exp, axis=-1)  32.5 us
    psum x1, waiting for transfers between devices, local(): projected = lax.psum(projected, 'head')  19.2 us
    psum x1, waiting for transfers between devices, local(): all_sums, all_totals = lax.psum((weighted, totals), 'exp')  17.7 us
    reduce_scatter x1, waiting for transfers between devices, local(): lax.psum_scatter(partial_value, 'head', scatter_dimension=3, tiled=True)  16.2 us
  transfers between devices with their start and end apart: 7, of which 7 were waited for; matrix products, arithmetic and copies ran while one was open for 11% of the time, Pallas kernels for 0%

profile of v1, /device:TPU:12, one launch (start us, length us, event | category | flops | bytes accessed | tf_op | source)
XLA Modules:
  0.0 444.5 jit_solution(2841263396190597828)
XLA Ops:
  6.5 1.2 copy.81
  7.7 1.2 stack.2
  8.9 4.2 all-to-all-start
  13.1 0.0 all-reduce.3.cloned.1.call-start
  13.1 0.1 broadcast_compare_fusion
  13.3 13.0 %all-to-all-done = bf16[4,4,16,16,128]{4,2,3,1,0:T(8,128)(2,1)S(1)} async-done(((bf16[4,4,16,16,128]{4,2,3,1,0:T(8,128)(2,1)}), bf16[4,4,16,16,128]{4,2,3,1,0:T(8,128)(2,1)S(1)}, u32[]{:S(2)}, u32[]{:S(2)}) %all-to-all-start) | async-done | bytes 1048608 | tf_op jit(solution)/shard_map/all_to_all | solution.py:36
  26.3 1.0 copy-done.2
  27.2 1.5 copy.82
  28.8 0.0 copy-done.7
  28.8 1.8 fusion.33
  30.5 43.4 %bitcast_reduce_fusion = (f32[4,2,8,64]{3,2,1,0:T(8,128)S(1)}, f32[4,2,6144,64,8]{2,3,4,1,0:T(8,128)}) fusion(pred[4,6144]{1,0:T(4,128)(4,1)S(1)} %broadcast_compare_fusion, bf16[4,64,2,8,128]{4,1,3,2,0:T(8,128)(2,1)S(1)} %bitcast.79, bf16[4,6144,2,128,1]{3,2,1,0,4:T(2,128)(2,1)} %bitcast.77), kind=kOutput, calls=%fused_computation.3 | convolution fusion | flops 6517944320 | bytes 114335744 | tf_op jit(solution)/shard_map/rbkgd,rskd->rkgbs/dot_general | solution.py:41
  73.9 15.3 %pmax.7 = f32[4,2,8,64]{3,2,1,0:T(8,128)S(1)} all-reduce(f32[4,2,8,64]{3,2,1,0:T(8,128)S(1)} %max.5), channel_id=1, replica_groups=mesh['req'=4,'head'=2,'exp'=4] {'exp'}, use_global_device_ids=true, to_apply=%region_2.3 | all-reduce | flops 4096 | bytes 32768 | tf_op jit(solution)/shard_map/pmax | solution.py:52
  89.2 0.0 copy-start.6
  89.3 38.4 %fusion.3 = f32[4,2,8,64,128]{4,3,2,1,0:T(8,128)} fusion(f32[4,2,6144,64,8]{2,3,4,1,0:T(8,128)} %get-tuple-element.10, f32[4,2,8,64]{3,2,1,0:T(8,128)S(1)} %pmax.7, pred[4,6144]{1,0:T(4,128)(4,1)S(1)} %broadcast_compare_fusion, bf16[4,6144,2,128,1]{3,2,1,0,4:T(2,128)(2,1)} %bitcast.85), kind=kOutput, calls=%fused_computation.8 | convolution fusion | flops 6543114240 | bytes 115384320 | tf_op jit(solution)/shard_map/rkgbs,rskd->rbkgd/dot_general | solution.py:56
  127.7 0.0 copy-done.1
  127.7 2.1 add_bitcast_fusion
  129.8 2.5 copy.87
  132.3 2.7 reshape.101
  135.0 0.0 all-reduce.3.cloned.1.call-update
  135.0 0.2 all-reduce.5.cloned.1.call-start
  135.3 32.4 %fusion.1 = f32[4,2,8,64]{3,2,1,0:T(8,128)S(1)} fusion(f32[4,2,6144,64,8]{2,3,4,1,0:T(8,128)} %get-tuple-element.10, f32[4,2,8,64]{3,2,1,0:T(8,128)S(1)} %pmax.7, pred[4,6144]{1,0:T(4,128)(4,1)S(1)} %broadcast_compare_fusion), kind=kLoop, calls=%fused_computation.6 | loop fusion | flops 100659200 | bytes 100720640 | tf_op jit(solution)/shard_map/reduce_sum | solution.py:55
  167.7 0.2 fusion.22
  167.8 14.9 %psum.22 = f32[4,64,16]{1,2,0:T(8,128)S(1)} all-reduce(f32[4,64,16]{1,2,0:T(8,128)S(1)} %add_bitcast_fusion.1), channel_id=1, replica_groups=mesh['req'=4,'head'=2,'exp'=4] {'exp'}, use_global_device_ids=true, to_apply=%region_6.7 | all-reduce | flops 4096 | bytes 32768 | tf_op jit(solution)/shard_map/psum | solution.py:70
  182.7 0.1 copy.88
  182.8 1.9 div.21
  184.8 2.7 div.22
  187.5 17.7 %all-reduce.3.cloned.1.call-done = f32[4,64,2048]{2,1,0:T(8,128)} async-done(((f32[4,64,2048]{2,1,0:T(8,128)}), f32[4,64,2048]{2,1,0:T(8,128)}) %all-reduce.3.cloned.1.call-update) | async-done | bytes 2097168 | tf_op jit(solution)/shard_map/psum | solution.py:70
  205.2 3.7 fusion.11
  208.9 0.0 all-reduce.5.cloned.1.call-update
  209.0 19.2 %all-reduce.5.cloned.1.call-done = f32[4,64,512]{2,1,0:T(8,128)} async-done(((f32[4,64,512]{2,1,0:T(8,128)}), f32[4,64,512]{2,1,0:T(8,128)}) %all-reduce.5.cloned.1.call-update) | async-done | bytes 524304 | tf_op jit(solution)/shard_map/psum | solution.py:76
  228.1 4.2 all-to-all-start.1
  232.3 0.1 copy.90
  232.4 0.1 reduce_window_sum.11
  232.5 0.1 copy.92
  232.6 0.1 reshape.118
  232.7 0.0 copy-start.4
  232.7 0.0 copy-start.8
  232.7 3.8 gather_fusion.1
  236.5 0.1 reshape.121
  236.6 0.1 copy.93
  236.7 0.1 copy.95
  236.8 0.7 fusion.13
  237.5 2.8 all-to-all-done.1
  240.3 0.2 multiply_reduce_fusion.1
  240.5 0.8 copy-done.3
  241.3 3.3 convolution_convert_fusion
  244.6 6.1 %all-to-all-start.2 = ((bf16[16,1,64,2048]{3,2,1,0:T(8,128)(2,1)}), bf16[16,1,64,2048]{3,2,1,0:T(8,128)(2,1)}, u32[]{:S(2)}, u32[]{:S(2)}) async-start(bf16[16,1,64,2048]{3,2,1,0:T(8,128)(2,1)} %bitcast.76), calls=%async_computation.2 | async-start | bytes 8388608 | tf_op jit(solution)/shard_map/all_to_all | solution.py:105
  250.7 0.0 reduce-scatter.2.cloned.1.call-start
  250.7 8.1 %reshape.136 = bf16[2048,768,1]{1,0,2:T(8,128)(2,1)} reshape(bf16[1,2048,2,384]{3,2,1,0:T(2,128)(2,1)} %param.24) | data formatting | bytes 6291456 | tf_op jit(solution)/shard_map/reshape.4
  258.8 84.6 %all-to-all-done.2 = bf16[16,1,64,2048]{3,2,1,0:T(8,128)(2,1)} async-done(((bf16[16,1,64,2048]{3,2,1,0:T(8,128)(2,1)}), bf16[16,1,64,2048]{3,2,1,0:T(8,128)(2,1)}, u32[]{:S(2)}, u32[]{:S(2)}) %all-to-all-start.2) | async-done | bytes 4194336 | tf_op jit(solution)/shard_map/all_to_all | solution.py:105
  343.4 6.3 %fusion.14 = f32[16,1,64,768]{3,2,0,1:T(8,128)S(1)} fusion(bf16[2048,768,1]{1,0,2:T(8,128)(2,1)} %reshape.136, bf16[16,1,64,2048]{3,2,1,0:T(8,128)(2,1)} %all-to-all-done.2), kind=kOutput, calls=%fused_computation.25 | convolution fusion | flops 3221225472 | bytes 10485760 | tf_op jit(solution)/shard_map/geci,eif->gecf/dot_general | solution.py:103
  349.7 5.6 %convolution_bitcast_fusion = f32[16,1,64,2048]{3,2,0,1:T(8,128)} fusion(bf16[1,384,2048]{2,1,0:T(8,128)(2,1)S(1)} %copy-done.11, f32[16,1,64,768]{3,2,0,1:T(8,128)S(1)} %fusion.14), kind=kOutput, calls=%fused_computation.13 | convolution fusion | flops 1612972032 | bytes 13107200 | tf_op jit(solution)/shard_map/gecf,efi->geci/dot_general | solution.py:113
  355.3 0.0 reduce-scatter.2.cloned.1.call-update
  355.3 16.2 %reduce-scatter.2.cloned.1.call-done = f32[16,1,64,1024]{3,2,0,1:T(8,128)} async-done(((f32[16,1,64,2048]{3,2,0,1:T(8,128)}), f32[16,1,64,1024]{3,2,0,1:T(8,128)}) %reduce-scatter.2.cloned.1.call-update) | async-done | bytes 4194320 | tf_op jit(solution)/shard_map/reduce_scatter | solution.py:118
  371.5 3.9 convert_bitcast_fusion
  375.4 7.1 %all-to-all-start.3 = ((bf16[16,1,64,1024]{3,2,1,0:T(8,128)(2,1)}), bf16[16,1,64,1024]{3,2,1,0:T(8,128)(2,1)}, u32[]{:S(2)}, u32[]{:S(2)}) async-start(bf16[16,1,64,1024]{3,2,1,0:T(8,128)(2,1)} %convert_bitcast_fusion), calls=%async_computation.4 | async-start | bytes 4194304 | tf_op jit(solution)/shard_map/all_to_all | solution.py:121
  382.5 0.1 copy.98
  382.6 0.1 reshape.112
  382.7 0.1 copy.94
  382.8 0.1 copy.99
  382.9 48.1 %all-to-all-done.3 = bf16[16,1,64,1024]{3,2,1,0:T(8,128)(2,1)} async-done(((bf16[16,1,64,1024]{3,2,1,0:T(8,128)(2,1)}), bf16[16,1,64,1024]{3,2,1,0:T(8,128)(2,1)}, u32[]{:S(2)}, u32[]{:S(2)}) %all-to-all-start.3) | async-done | bytes 2097184 | tf_op jit(solution)/shard_map/all_to_all | solution.py:121
  431.0 4.6 %gather_fusion = bf16[512,1024]{1,0:T(8,128)(2,1)S(1)} fusion(bf16[1024,1024]{1,0:T(8,128)(2,1)} %bitcast.29, s32[1024]{0:T(1024)S(1)} %pad_clamp_fusion), kind=kCustom, calls=%fused_computation | custom fusion | bytes 2099200 | tf_op jit(solution)/shard_map/jit(_take)/gather | solution.py:123
  435.5 0.8 multiply_reduce_fusion
  436.4 1.6 add_convert_fusion
  (28 shorter events, 0.1 us)
Async XLA Ops:
  6.5 198.6 %copy-start = (bf16[2048,512]{1,0:T(8,128)(2,1)S(1)}, bf16[2048,512]{1,0:T(8,128)(2,1)}, u32[]{:S(2)}) copy-start(bf16[2048,512]{1,0:T(8,128)(2,1)} %param.20) | copy-start | bytes 6291460
  6.5 6.6 %copy-start.10 = (s32[4]{0:T(128)S(1)}, s32[4]{0:T(128)}, u32[]{:S(2)}) copy-start(s32[4]{0:T(128)} %param.18) | copy-start | bytes 52
  6.5 22.2 %copy-start.7 = (bf16[4,16,2,128]{3,2,1,0:T(2,128)(2,1)S(1)}, bf16[4,16,2,128]{3,2,1,0:T(2,128)(2,1)}, u32[]{:S(2)}) copy-start(bf16[4,16,2,128]{3,2,1,0:T(2,128)(2,1)} %param.14) | copy-start | bytes 98308
  8.9 17.4 %all-to-all-start = ((bf16[4,4,16,16,128]{4,2,3,1,0:T(8,128)(2,1)}), bf16[4,4,16,16,128]{4,2,3,1,0:T(8,128)(2,1)S(1)}, u32[]{:S(2)}, u32[]{:S(2)}) async-start(bf16[4,4,16,16,128]{4,2,3,1,0:T(8,128)(2,1)} %stack.2), calls=%async_computation | async-start | bytes 2097152 | tf_op jit(solution)/shard_map/all_to_all | solution.py:36
  13.1 192.0 %all-reduce.3.cloned.1.call-start = ((), (), s32[]{:S(2)}) async-start(), calls=%async_computation.5 | async-start | bytes 4194304 | tf_op jit(solution)/shard_map/psum | solution.py:70
  26.3 1.0 copy-start.2
  89.2 38.4 %copy-start.1 = (f32[4,2,8,64,16]{3,4,2,1,0:T(8,128)S(1)}, f32[4,2,8,64,16]{3,4,2,1,0:T(8,128)}, u32[]{:S(2)}) copy-start(f32[4,2,8,64,16]{3,4,2,1,0:T(8,128)} %get-tuple-element.12) | copy-start | bytes 786436
  89.2 38.4 %copy-start.6 = (bf16[4,16,2,128]{3,2,1,0:T(2,128)(2,1)S(1)}, bf16[4,16,2,128]{3,2,1,0:T(2,128)(2,1)}, u32[]{:S(2)}) copy-start(bf16[4,16,2,128]{3,2,1,0:T(2,128)(2,1)} %param.15) | copy-start | bytes 98308
  135.0 93.1 %all-reduce.5.cloned.1.call-start = ((), (), s32[]{:S(2)}) async-start(), calls=%async_computation.6 | async-start | bytes 1048576 | tf_op jit(solution)/shard_map/psum | solution.py:76
  187.5 21.4 %copy-start.5 = (s32[64,8]{0,1:T(8,128)S(1)}, s32[64,8]{0,1:T(8,128)}, u32[]{:S(2)}) copy-start(s32[64,8]{0,1:T(8,128)} %param.22) | copy-start | bytes 6148
  228.1 12.2 %all-to-all-start.1 = ((f32[4,64,512]{2,1,0:T(8,128)}), f32[4,64,512]{2,1,0:T(8,128)S(1)}, u32[]{:S(2)}, u32[]{:S(2)}) async-start(f32[4,64,512]{2,1,0:T(8,128)} %all-reduce.5.cloned.1.call-done), calls=%async_computation.1 | async-start | bytes 1048576 | tf_op jit(solution)/shard_map/all_to_all | solution.py:78
  232.7 7.6 %copy-start.4 = (bf16[64,2048]{1,0:T(8,128)(2,1)S(1)}, bf16[64,2048]{1,0:T(8,128)(2,1)}, u32[]{:S(2)}) copy-start(bf16[64,2048]{1,0:T(8,128)(2,1)} %param.19) | copy-start | bytes 786436
  232.7 8.6 %copy-start.8 = (f32[2048]{0:T(1024)S(1)}, f32[2048]{0:T(1024)}, u32[]{:S(2)}) copy-start(f32[2048]{0:T(1024)} %param.21) | copy-start | bytes 24580
  240.5 0.8 copy-start.3
  244.6 98.8 %all-to-all-start.2 = ((bf16[16,1,64,2048]{3,2,1,0:T(8,128)(2,1)}), bf16[16,1,64,2048]{3,2,1,0:T(8,128)(2,1)}, u32[]{:S(2)}, u32[]{:S(2)}) async-start(bf16[16,1,64,2048]{3,2,1,0:T(8,128)(2,1)} %bitcast.76), calls=%async_computation.2 | async-start | bytes 8388608 | tf_op jit(solution)/shard_map/all_to_all | solution.py:105
  250.7 120.8 %reduce-scatter.2.cloned.1.call-start = ((), (), s32[]{:S(2)}) async-start(), calls=%async_computation.7 | async-start | bytes 12582912 | tf_op jit(solution)/shard_map/reduce_scatter | solution.py:118
  343.4 6.3 %copy-start.11 = (bf16[1,384,2048]{2,1,0:T(8,128)(2,1)S(1)}, bf16[1,384,2048]{2,1,0:T(8,128)(2,1)}, u32[]{:S(2)}) copy-start(bf16[1,384,2048]{2,1,0:T(8,128)(2,1)} %param.25) | copy-start | bytes 4718596
  375.4 7.4 %copy-start.9 = (f32[64,8]{0,1:T(8,128)S(1)}, f32[64,8]{0,1:T(8,128)}, u32[]{:S(2)}) copy-start(f32[64,8]{0,1:T(8,128)} %param.23) | copy-start | bytes 6148
  375.4 55.6 %all-to-all-start.3 = ((bf16[16,1,64,1024]{3,2,1,0:T(8,128)(2,1)}), bf16[16,1,64,1024]{3,2,1,0:T(8,128)(2,1)}, u32[]{:S(2)}, u32[]{:S(2)}) async-start(bf16[16,1,64,1024]{3,2,1,0:T(8,128)(2,1)} %convert_bitcast_fusion), calls=%async_computation.4 | async-start | bytes 4194304 | tf_op jit(solution)/shard_map/all_to_all | solution.py:121
Sparse Core Ops, SparseCore 0:
  135.2 69.9 all-reduce.2
  209.1 19.0 all-reduce.4
  355.5 15.9 reduce-scatter.1
